TPU v7x, 32 devices: a whole 2x2x4 slice. The times are simulated.
32 devices in a mesh: gx: 4 (over y, x), gy: 8 (over z, core).
Axes of the slice: x: 2, y: 2, z: 4, core: 2. Of those that a mesh axis runs over, the one named last changes fastest.
Arguments:
- grad_out: bfloat16 [16, 16, 64, 256], P('gx', 'gy'), may hold values from -6 to 6
- relu_mask: int32 [16, 16, 64, 256], P('gx', 'gy'), may hold values 0 or 1
- activations: bfloat16 [16, 16, 64, 256], P('gx', 'gy'), may hold values from -6 to 6
- weight: bfloat16 [27, 256, 256], P(None, 'gx'), may hold values from -0.078125 to 0.078125
Outputs:
- grad_input: bfloat16 [16, 16, 64, 256], P('gx', 'gy')
- weight_grad: float32 [27, 256, 256], P(None, 'gx', 'gy')
All inputs are finite; a program needn't handle non-finite values. No bound on the sum of `relu_mask` on one device may be relied on, other than what follows from the above.
Results may differ from a plain program's by a relative error of at most 0.001.
Values may be sent and summed in bfloat16 or wider, within the bound.
A program may use at most 64 MiB of HBM per device.

v0:
```python
import math
import jax
import jax.numpy as jnp
from jax import lax
from jax.sharding import PartitionSpec as P


def padded(shard, sides, width):
    for axis, dim in sides:
        devices, length = (lax.axis_size(axis), shard.shape[dim])
        up = [(i, (i + 1) % devices) for i in range(devices - 1)]
        down = [(j, i) for i, j in up]
        last = lax.slice_in_dim(shard, length - width, length, axis=dim)
        leading = lax.slice_in_dim(shard, 0, width, axis=dim)
        before = lax.ppermute(last, axis, up)
        after = lax.ppermute(leading, axis, down)
        shard = jnp.concatenate([before, shard, after], axis=dim)
    return shard


def tap_list():
    return [(a, b, c) for a in (-1, 0, 1) for b in (-1, 0, 1) for c in (-1, 0, 1)]


def body(grad_out, relu_mask, activations, weight):
    size_x, size_y, size_z = (grad_out.shape[0], grad_out.shape[1], grad_out.shape[2])
    out_chan = grad_out.shape[3]
    in_chan = activations.shape[3]
    cells = size_x * size_y * size_z
    gated = jnp.where(relu_mask != 0, grad_out, jnp.zeros_like(grad_out))
    grad_cycle = padded(gated, (("gx", 0), ("gy", 1)), 1)
    grad_pad = jnp.pad(grad_cycle, ((0, 0), (0, 0), (1, 1), (0, 0)))
    input_cycle = padded(activations, (("gx", 0), ("gy", 1)), 1)
    input_pad = jnp.pad(input_cycle, ((0, 0), (0, 0), (1, 1), (0, 0)))
    piece = lax.all_gather(weight, "gx", axis=1, tiled=True)
    accum = jnp.zeros((cells, piece.shape[1]), jnp.float32)
    for tap, (project_a, project_b, project_c) in enumerate(tap_list()):
        window = grad_pad[
            1 - project_a : 1 - project_a + size_x,
            1 - project_b : 1 - project_b + size_y,
            1 - project_c : 1 - project_c + size_z,
            :,
        ].reshape(cells, out_chan)
        accum = accum + lax.dot_general(
            window, piece[tap], (((1,), (1,)), ((), ())), preferred_element_type=jnp.float32
        )
    grad_input = accum.reshape(size_x, size_y, size_z, piece.shape[1]).astype(jnp.bfloat16)
    gated_flat = gated.reshape(cells, out_chan)
    terms = []
    for a, b, c in tap_list():
        shifted = input_pad[
            1 + a : 1 + a + size_x, 1 + b : 1 + b + size_y, 1 + c : 1 + c + size_z, :
        ].reshape(cells, in_chan)
        terms.append(
            lax.dot_general(
                shifted, gated_flat, (((0,), (0,)), ((), ())), preferred_element_type=jnp.float32
            )
        )
    partial_value = jnp.stack(terms, axis=0)[None]
    pieces = lax.all_to_all(partial_value, "gy", split_axis=3, concat_axis=0, tiled=True)
    section = jnp.sum(pieces, axis=0)
    summed = lax.psum_scatter(section, "gx", scatter_dimension=1, tiled=True)
    whole_cells = cells * lax.axis_size("gx") * lax.axis_size("gy")
    weight_grad = summed * (1.0 / math.sqrt(whole_cells))
    return (grad_input, weight_grad)


def solution(mesh):
    in_specs = (
        P("gx", "gy", None, None),
        P("gx", "gy", None, None),
        P("gx", "gy", None, None),
        P(None, "gx", None),
    )
    out_specs = (P("gx", "gy", None, None), P(None, "gx", "gy"))
    return jax.shard_map(body, mesh=mesh, in_specs=in_specs, out_specs=out_specs, check_vma=False)
```

profile of v0, /device:TPU:0, one launch (start us, length us, event | category | flops | bytes accessed | tf_op | source)
XLA Modules:
  0.0 302.3 jit_solution(12069150072496918049)
XLA Ops:
  8.0 4.9 %collective-permute-start.4 = (bf16[1,2,64,256]{3,2,1,0:T(8,128)(2,1)S(1)}, bf16[1,2,64,256]{3,2,1,0:T(8,128)(2,1)S(1)}, u32[]{:S(2)}, u32[]{:S(2)}) collective-permute-start(bf16[1,2,64,256]{3,2,1,0:T(8,128)(2,1)S(1)} %get-tuple-element.33), channel_id=1, source_target_pairs={{0,8},{8,16},{16,24},{1,9},{9,17},{17,25},{2,10},{10,18},{18,26},{... | collective-permute-start | bytes 196616 | tf_op jit(solution)/shard_map/ppermute | solution.py:15
  12.9 1.3 collective-permute-start.5
  15.8 3.3 %collective-permute-done.5 = bf16[1,2,64,256]{3,2,1,0:T(8,128)(2,1)S(1)} collective-permute-done((bf16[1,2,64,256]{3,2,1,0:T(8,128)(2,1)S(1)}, bf16[1,2,64,256]{3,2,1,0:T(8,128)(2,1)S(1)}, u32[]{:S(2)}, u32[]{:S(2)}) %collective-permute-start.5) | collective-permute-done | bytes 65568 | tf_op jit(solution)/shard_map/ppermute | solution.py:16
  19.1 1.3 collective-permute-start.6
  20.4 1.4 collective-permute-start.7
  21.9 1.2 compare_select_fusion
  23.1 2.6 collective-permute-done.7
  29.1 1.0 fusion.28
  32.0 1.0 fusion.26
  34.0 1.0 fusion.25
  35.0 1.0 fusion.24
  36.0 1.0 fusion.8
  42.8 1.0 fusion.18
  43.8 1.0 fusion.17
  44.8 1.0 fusion.6
  45.8 1.0 fusion.16
  46.8 1.0 fusion.15
  47.8 1.0 fusion.5
  49.7 1.0 fusion.13
  52.7 16.9 %copy.13 = f32[1,27,256,256]{2,0,1,3:T(1,128)} copy(f32[1,27,256,256]{3,2,1,0:T(8,128)} %bitcast.136) | data formatting | bytes 14155776 | tf_op jit(solution)/shard_map/broadcast_in_dim | solution.py:59
  69.5 7.6 %all-to-all-start = ((f32[1,27,256,256]{2,0,1,3:T(1,128)}), f32[1,27,256,256]{2,0,1,3:T(1,128)}, u32[]{:S(2)}, u32[]{:S(2)}) async-start(f32[1,27,256,256]{2,0,1,3:T(1,128)} %copy.13), calls=%async_computation | async-start | bytes 14155776 | tf_op jit(solution)/shard_map/all_to_all | solution.py:60
  78.0 4.3 %collective-permute-start = (bf16[1,2,64,256]{3,2,1,0:T(8,128)(2,1)S(1)}, bf16[1,2,64,256]{3,2,1,0:T(8,128)(2,1)S(1)}, u32[]{:S(2)}, u32[]{:S(2)}) collective-permute-start(bf16[1,2,64,256]{3,2,1,0:T(8,128)(2,1)S(1)} %get-tuple-element.36), channel_id=1, source_target_pairs={{0,8},{8,16},{16,24},{1,9},{9,17},{17,25},{2,10},{10,18},{18,26},{... | collective-permute-start | bytes 196616 | tf_op jit(solution)/shard_map/ppermute | solution.py:15
  82.3 1.3 collective-permute-start.1
  84.4 4.7 %collective-permute-done.1 = bf16[1,2,64,256]{3,2,1,0:T(8,128)(2,1)S(1)} collective-permute-done((bf16[1,2,64,256]{3,2,1,0:T(8,128)(2,1)S(1)}, bf16[1,2,64,256]{3,2,1,0:T(8,128)(2,1)S(1)}, u32[]{:S(2)}, u32[]{:S(2)}) %collective-permute-start.1) | collective-permute-done | bytes 65568 | tf_op jit(solution)/shard_map/ppermute | solution.py:16
  89.2 2.2 collective-permute-start.2
  91.4 1.5 collective-permute-start.3
  92.9 2.8 collective-permute-done.3
  96.3 1.0 fusion.72
  97.3 1.9 fusion.71
  99.1 29.2 %all-gather.2.cloned.1.call-done = bf16[27,256,256]{2,1,0:T(8,128)(2,1)} async-done(((bf16[27,64,256]{2,1,0:T(8,128)(2,1)}), bf16[27,256,256]{2,1,0:T(8,128)(2,1)}) %all-gather.2.cloned.1.call-update) | async-done | bytes 3538960 | tf_op jit(solution)/shard_map/all_gather | solution.py:35
  128.4 1.3 fusion.62
  129.7 1.2 fusion.61
  130.9 1.3 convolution_add_fusion.23
  132.2 1.3 convolution_add_fusion.22
  138.0 95.4 %all-to-all-done = f32[1,27,256,256]{2,0,1,3:T(1,128)} async-done(((f32[1,27,256,256]{2,0,1,3:T(1,128)}), f32[1,27,256,256]{2,0,1,3:T(1,128)}, u32[]{:S(2)}, u32[]{:S(2)}) %all-to-all-start) | async-done | bytes 7077920 | tf_op jit(solution)/shard_map/all_to_all | solution.py:60
  233.4 6.8 %copy.14 = f32[1,27,256,256]{2,3,1,0:T(8,128)} copy(f32[1,27,256,256]{2,0,1,3:T(1,128)} %all-to-all-done) | data formatting | bytes 14155776 | tf_op jit(solution)/shard_map/all_to_all | solution.py:60
  240.2 3.9 %reduce_sum.9 = f32[27,256,32]{1,2,0:T(8,128)S(1)} reduce(f32[27,256,8,32]{1,3,2,0:T(8,128)} %bitcast.385, f32[]{:T(128)} %constant.2.clone.1), dimensions={2}, to_apply=%region_0.1 | reduce | flops 1548288 | bytes 7962628 | tf_op jit(solution)/shard_map/reduce_sum | solution.py:61
  244.1 4.4 %copy.43 = f32[27,256,32]{2,0,1:T(8,128)} copy(f32[27,256,32]{1,2,0:T(8,128)S(1)} %reduce_sum.9) | data formatting | bytes 1769472
  248.5 4.2 %reshape.170 = f32[256,864]{1,0:T(8,128)} reshape(f32[256,27,32]{2,1,0:T(8,128)} %bitcast.386) | data formatting | bytes 1769472
  252.7 1.2 fusion.60
  253.9 1.2 convolution_add_fusion.5
  255.0 1.2 convolution_add_fusion.4
  256.2 1.2 fusion.1
  257.4 1.2 convolution_add_fusion.2
  258.6 1.2 convolution_add_fusion.1
  259.7 1.9 fusion.3
  261.6 31.3 %reduce-scatter.4.cloned.1.call-done = f32[64,864]{1,0:T(8,128)} async-done(((f32[256,864]{1,0:T(8,128)}), f32[64,864]{1,0:T(8,128)}) %reduce-scatter.4.cloned.1.call-update) | async-done | bytes 221200
  292.9 1.3 reshape.171
  (81 shorter events, 25.3 us)
Async XLA Ops:
  8.0 6.8 %collective-permute-start.4 = (bf16[1,2,64,256]{3,2,1,0:T(8,128)(2,1)S(1)}, bf16[1,2,64,256]{3,2,1,0:T(8,128)(2,1)S(1)}, u32[]{:S(2)}, u32[]{:S(2)}) collective-permute-start(bf16[1,2,64,256]{3,2,1,0:T(8,128)(2,1)S(1)} %get-tuple-element.33), channel_id=1, source_target_pairs={{0,8},{8,16},{16,24},{1,9},{9,17},{17,25},{2,10},{10,18},{18,26},{... | collective-permute-start | bytes 196616 | tf_op jit(solution)/shard_map/ppermute | solution.py:15
  12.9 6.2 %collective-permute-start.5 = (bf16[1,2,64,256]{3,2,1,0:T(8,128)(2,1)S(1)}, bf16[1,2,64,256]{3,2,1,0:T(8,128)(2,1)S(1)}, u32[]{:S(2)}, u32[]{:S(2)}) collective-permute-start(bf16[1,2,64,256]{3,2,1,0:T(8,128)(2,1)S(1)} %get-tuple-element.32), channel_id=1, source_target_pairs={{8,0},{16,8},{24,16},{9,1},{17,9},{25,17},{10,2},{18,10},{26,18},{... | collective-permute-start | bytes 196616 | tf_op jit(solution)/shard_map/ppermute | solution.py:16
  19.1 3.9 %collective-permute-start.6 = (bf16[6,1,64,256]{3,2,1,0:T(8,128)(2,1)S(1)}, bf16[6,1,64,256]{3,2,1,0:T(8,128)(2,1)S(1)}, u32[]{:S(2)}, u32[]{:S(2)}) collective-permute-start(bf16[6,1,64,256]{3,2,1,0:T(8,128)(2,1)S(1)} %get-tuple-element.26), channel_id=1, source_target_pairs={{0,1},{1,2},{2,3},{3,4},{4,5},{5,6},{6,7},{8,9},{9,10},{10,11},{11... | collective-permute-start | bytes 589832 | tf_op jit(solution)/shard_map/ppermute | solution.py:15
  20.4 9.6 %copy-start.1 = (bf16[4,2,64,256]{3,2,1,0:T(8,128)(2,1)S(1)}, bf16[4,2,64,256]{3,2,1,0:T(8,128)(2,1)}, u32[]{:S(2)}) copy-start(bf16[4,2,64,256]{3,2,1,0:T(8,128)(2,1)} %param.6) | copy-start | bytes 786436
  20.4 5.3 %collective-permute-start.7 = (bf16[6,1,64,256]{3,2,1,0:T(8,128)(2,1)S(1)}, bf16[6,1,64,256]{3,2,1,0:T(8,128)(2,1)S(1)}, u32[]{:S(2)}, u32[]{:S(2)}) collective-permute-start(bf16[6,1,64,256]{3,2,1,0:T(8,128)(2,1)S(1)} %get-tuple-element.27), channel_id=1, source_target_pairs={{1,0},{2,1},{3,2},{4,3},{5,4},{6,5},{7,6},{9,8},{10,9},{11,10},{12... | collective-permute-start | bytes 589832 | tf_op jit(solution)/shard_map/ppermute | solution.py:16
  69.5 163.8 %all-to-all-start = ((f32[1,27,256,256]{2,0,1,3:T(1,128)}), f32[1,27,256,256]{2,0,1,3:T(1,128)}, u32[]{:S(2)}, u32[]{:S(2)}) async-start(f32[1,27,256,256]{2,0,1,3:T(1,128)} %copy.13), calls=%async_computation | async-start | bytes 14155776 | tf_op jit(solution)/shard_map/all_to_all | solution.py:60
  77.2 51.2 %all-gather.2.cloned.1.call-start = ((), (), s32[]{:S(2)}) async-start(), calls=%async_computation.2 | async-start | bytes 4423680 | tf_op jit(solution)/shard_map/all_gather | solution.py:35
  77.9 215.0 %reduce-scatter.4.cloned.1.call-start = ((), (), s32[]{:S(2)}) async-start(), calls=%async_computation.3 | async-start | bytes 1146880
  78.0 6.4 %collective-permute-start = (bf16[1,2,64,256]{3,2,1,0:T(8,128)(2,1)S(1)}, bf16[1,2,64,256]{3,2,1,0:T(8,128)(2,1)S(1)}, u32[]{:S(2)}, u32[]{:S(2)}) collective-permute-start(bf16[1,2,64,256]{3,2,1,0:T(8,128)(2,1)S(1)} %get-tuple-element.36), channel_id=1, source_target_pairs={{0,8},{8,16},{16,24},{1,9},{9,17},{17,25},{2,10},{10,18},{18,26},{... | collective-permute-start | bytes 196616 | tf_op jit(solution)/shard_map/ppermute | solution.py:15
  82.3 6.8 %collective-permute-start.1 = (bf16[1,2,64,256]{3,2,1,0:T(8,128)(2,1)S(1)}, bf16[1,2,64,256]{3,2,1,0:T(8,128)(2,1)S(1)}, u32[]{:S(2)}, u32[]{:S(2)}) collective-permute-start(bf16[1,2,64,256]{3,2,1,0:T(8,128)(2,1)S(1)} %get-tuple-element.37), channel_id=1, source_target_pairs={{8,0},{16,8},{24,16},{9,1},{17,9},{25,17},{10,2},{18,10},{26,18},{... | collective-permute-start | bytes 196616 | tf_op jit(solution)/shard_map/ppermute | solution.py:16
  89.2 3.7 %collective-permute-start.2 = (bf16[6,1,64,256]{3,2,1,0:T(8,128)(2,1)S(1)}, bf16[6,1,64,256]{3,2,1,0:T(8,128)(2,1)S(1)}, u32[]{:S(2)}, u32[]{:S(2)}) collective-permute-start(bf16[6,1,64,256]{3,2,1,0:T(8,128)(2,1)S(1)} %get-tuple-element.30), channel_id=1, source_target_pairs={{0,1},{1,2},{2,3},{3,4},{4,5},{5,6},{6,7},{8,9},{9,10},{10,11},{11... | collective-permute-start | bytes 589832 | tf_op jit(solution)/shard_map/ppermute | solution.py:15
  91.4 4.3 %collective-permute-start.3 = (bf16[6,1,64,256]{3,2,1,0:T(8,128)(2,1)S(1)}, bf16[6,1,64,256]{3,2,1,0:T(8,128)(2,1)S(1)}, u32[]{:S(2)}, u32[]{:S(2)}) collective-permute-start(bf16[6,1,64,256]{3,2,1,0:T(8,128)(2,1)S(1)} %get-tuple-element.31), channel_id=1, source_target_pairs={{1,0},{2,1},{3,2},{4,3},{5,4},{6,5},{7,6},{9,8},{10,9},{11,10},{12... | collective-permute-start | bytes 589832 | tf_op jit(solution)/shard_map/ppermute | solution.py:16
  128.4 5.1 %copy-start = (bf16[27,256,256]{2,1,0:T(8,128)(2,1)S(1)}, bf16[27,256,256]{2,1,0:T(8,128)(2,1)}, u32[]{:S(2)}) copy-start(bf16[27,256,256]{2,1,0:T(8,128)(2,1)} %all-gather.2.cloned.1.call-done) | copy-start | bytes 10616836
  128.4 5.1 %copy-start.13 = (bf16[4,2,64,256]{3,2,1,0:T(8,128)(2,1)S(1)}, bf16[4,2,64,256]{3,2,1,0:T(8,128)(2,1)}, u32[]{:S(2)}) copy-start(bf16[4,2,64,256]{3,2,1,0:T(8,128)(2,1)} %get-tuple-element.17) | copy-start | bytes 786436
  129.7 4.4 %copy-start.12 = (bf16[4,2,64,256]{3,2,1,0:T(8,128)(2,1)S(1)}, bf16[4,2,64,256]{3,2,1,0:T(8,128)(2,1)}, u32[]{:S(2)}) copy-start(bf16[4,2,64,256]{3,2,1,0:T(8,128)(2,1)} %get-tuple-element.15) | copy-start | bytes 786436
  130.9 3.5 %copy-start.7 = (bf16[4,2,64,256]{3,2,1,0:T(8,128)(2,1)S(1)}, bf16[4,2,64,256]{3,2,1,0:T(8,128)(2,1)}, u32[]{:S(2)}) copy-start(bf16[4,2,64,256]{3,2,1,0:T(8,128)(2,1)} %get-tuple-element.22) | copy-start | bytes 786436
  132.2 2.5 copy-start.11
  133.5 1.4 copy-start.10
  133.8 1.4 copy-start.4
  134.1 1.4 copy-start.9
  134.4 1.4 copy-start.8
  134.9 1.4 copy-start.6
  135.2 1.4 copy-start.5
  135.8 1.4 copy-start.3
  136.1 1.4 copy-start.2
Sparse Core Ops, SparseCore 0:
  79.8 48.5 all-gather.1
  252.8 39.9 reduce-scatter.3
where the time goes:
time: 304 us; the launch traced here: 302 us
  waiting for transfers between devices  171 us (56%)
  matrix products  44.5 us (15%)
  local copies, waits for them, and re-layouts  39 us (13%)
  starting transfers between devices  25.8 us (8%)
  between operations  14.6 us (5%)
  other arithmetic  7.02 us (2%)
    all_to_all x1, waiting for transfers between devices, body(): lax.all_to_all(partial_value, 'gy', split_axis=3, concat_axis=0, tiled=True)  95.4 us
    unnamed x3, waiting for transfers between devices  32 us
    all_gather x1, waiting for transfers between devices, body(): piece = lax.all_gather(weight, 'gx', axis=1, tiled=True)  29.2 us
    dot_general x27, matrix products, body(): lax.dot_general(shifted, gated_flat, (((0,), (0,)), ((), ())), preferred_...  26.5 us
    dot_general x27, matrix products, body(): lax.dot_general(window, piece[tap], (((1,), (1,)), ((), ())), preferred_e...  18.1 us
    broadcast_in_dim x1, local copies, waits for them, and re-layouts, body(): partial_value = jnp.stack(terms, axis=0)[None]  16.9 us
    ppermute x4, waiting for transfers between devices, padded(): after = lax.ppermute(leading, axis, down)  13.4 us
    ppermute x4, starting transfers between devices, padded(): before = lax.ppermute(last, axis, up)  12.7 us
  transfers between devices with their start and end apart: 11, of which 9 were waited for; matrix products, arithmetic and copies ran while one was open for 8% of the time, Pallas kernels for 0%

commit v1 on v0

--- a/solution.py
+++ b/solution.py
@@ -57,7 +57,12 @@
             )
         )
     partial_value = jnp.stack(terms, axis=0)[None]
-    pieces = lax.all_to_all(partial_value, "gy", split_axis=3, concat_axis=0, tiled=True)
+    pieces = jnp.concatenate(
+        lax.all_to_all(
+            jnp.stack(jnp.split(partial_value, lax.axis_size("gy"), axis=3)), "gy", 0, 0
+        ),
+        axis=0,
+    )
     section = jnp.sum(pieces, axis=0)
     summed = lax.psum_scatter(section, "gx", scatter_dimension=1, tiled=True)
     whole_cells = cells * lax.axis_size("gx") * lax.axis_size("gy")

time: 304 us -> 271 us (0.89)
  matrix products: 44.5 us -> 27.7 us
  local copies, waits for them, and re-layouts: 39 us -> 23.7 us
    dot_general x27, matrix products: 26.5 us -> 7.63 us  [body(): lax.dot_general(shifted, gated_flat, (((0,), (0,)), ((), ())), preferred_...]
    broadcast_in_dim x1 -> x0, local copies, waits for them, and re-layouts: 16.9 us -> none  [body(): partial_value = jnp.stack(terms, axis=0)[None]]
    unnamed x34 -> x39, local copies, waits for them, and re-layouts: 11.5 us -> 18.5 us
    all_to_all x1 -> x0, local copies, waits for them, and re-layouts: 6.83 us -> none  [body(): lax.all_to_all(partial_value, 'gy', split_axis=3, concat_axis=0, tiled=True)]
  transfers between devices with their start and end apart: 11 -> 11, of which waited for: 9 -> 9; matrix products, arithmetic and copies ran while one was open for 8% -> 10% of each run, Pallas kernels for 0% -> 0%
where the time goes in v1:
time: 271 us; the launch traced here: 270 us
  waiting for transfers between devices  171 us (63%)
  matrix products  27.7 us (10%)
  starting transfers between devices  25.7 us (9%)
  local copies, waits for them, and re-layouts  23.7 us (9%)
  between operations  14.6 us (5%)
  other arithmetic  6.92 us (3%)
    all_to_all x1, waiting for transfers between devices, body(): lax.all_to_all(jnp.stack(jnp.split(partial_value, lax.axis_size('gy'), ax...  93.4 us
    unnamed x3, waiting for transfers between devices  34.2 us
    all_gather x1, waiting for transfers between devices, body(): piece = lax.all_gather(weight, 'gx', axis=1, tiled=True)  29 us
    dot_general x27, matrix products, body(): lax.dot_general(window, piece[tap], (((1,), (1,)), ((), ())), preferred_e...  20.1 us
    unnamed x39, local copies, waits for them, and re-layouts  18.5 us
    ppermute x4, waiting for transfers between devices, padded(): after = lax.ppermute(leading, axis, down)  13.4 us
    ppermute x4, starting transfers between devices, padded(): before = lax.ppermute(last, axis, up)  12.7 us
    dot_general x27, matrix products, body(): lax.dot_general(shifted, gated_flat, (((0,), (0,)), ((), ())), preferred_...  7.63 us
  transfers between devices with their start and end apart: 11, of which 9 were waited for; matrix products, arithmetic and copies ran while one was open for 10% of the time, Pallas kernels for 0%

profile of v1, /device:TPU:0, one launch (start us, length us, event | category | flops | bytes accessed | tf_op | source)
XLA Modules:
  0.0 270.0 jit_solution(8340023863182563140)
XLA Ops:
  7.2 0.9 fusion.84
  8.1 4.9 %collective-permute-start.4 = (bf16[1,2,64,256]{3,2,1,0:T(8,128)(2,1)S(1)}, bf16[1,2,64,256]{3,2,1,0:T(8,128)(2,1)S(1)}, u32[]{:S(2)}, u32[]{:S(2)}) collective-permute-start(bf16[1,2,64,256]{3,2,1,0:T(8,128)(2,1)S(1)} %get-tuple-element.33), channel_id=1, source_target_pairs={{0,8},{8,16},{16,24},{1,9},{9,17},{17,25},{2,10},{10,18},{18,26},{... | collective-permute-start | bytes 196616 | tf_op jit(solution)/shard_map/ppermute | solution.py:15
  13.0 1.3 collective-permute-start.5
  14.9 1.0 constant_dynamic-update-slice_fusion.1
  15.8 3.3 %collective-permute-done.5 = bf16[1,2,64,256]{3,2,1,0:T(8,128)(2,1)S(1)} collective-permute-done((bf16[1,2,64,256]{3,2,1,0:T(8,128)(2,1)S(1)}, bf16[1,2,64,256]{3,2,1,0:T(8,128)(2,1)S(1)}, u32[]{:S(2)}, u32[]{:S(2)}) %collective-permute-start.5) | collective-permute-done | bytes 65568 | tf_op jit(solution)/shard_map/ppermute | solution.py:16
  19.2 1.3 collective-permute-start.6
  20.5 1.3 collective-permute-start.7
  21.8 1.2 compare_select_fusion
  23.0 2.6 collective-permute-done.7
  33.8 1.0 fusion.38
  34.8 1.0 fusion.37
  35.9 1.0 fusion.36
  36.9 1.0 fusion.35
  37.9 1.0 fusion.34
  38.9 1.0 fusion.33
  39.9 1.1 fusion.32
  40.9 1.0 fusion.31
  41.9 7.6 %all-to-all-start = ((f32[8,1,27,256,32]{3,4,2,1,0:T(8,128)}), f32[8,1,27,256,32]{3,4,2,1,0:T(8,128)}, u32[]{:S(2)}, u32[]{:S(2)}) async-start(f32[8,1,27,256,32]{3,4,2,1,0:T(8,128)} %fusion.31), calls=%async_computation | async-start | bytes 14155776 | tf_op jit(solution)/shard_map/all_to_all | solution.py:61
  50.3 4.3 %collective-permute-start = (bf16[1,2,64,256]{3,2,1,0:T(8,128)(2,1)S(1)}, bf16[1,2,64,256]{3,2,1,0:T(8,128)(2,1)S(1)}, u32[]{:S(2)}, u32[]{:S(2)}) collective-permute-start(bf16[1,2,64,256]{3,2,1,0:T(8,128)(2,1)S(1)} %get-tuple-element.36), channel_id=1, source_target_pairs={{0,8},{8,16},{16,24},{1,9},{9,17},{17,25},{2,10},{10,18},{18,26},{... | collective-permute-start | bytes 196616 | tf_op jit(solution)/shard_map/ppermute | solution.py:15
  54.6 1.3 collective-permute-start.1
  55.9 0.8 collective-permute-done
  56.8 4.7 %collective-permute-done.1 = bf16[1,2,64,256]{3,2,1,0:T(8,128)(2,1)S(1)} collective-permute-done((bf16[1,2,64,256]{3,2,1,0:T(8,128)(2,1)S(1)}, bf16[1,2,64,256]{3,2,1,0:T(8,128)(2,1)S(1)}, u32[]{:S(2)}, u32[]{:S(2)}) %collective-permute-start.1) | collective-permute-done | bytes 65568 | tf_op jit(solution)/shard_map/ppermute | solution.py:16
  61.5 2.2 collective-permute-start.2
  63.7 1.5 collective-permute-start.3
  65.3 2.8 %collective-permute-done.3 = bf16[6,1,64,256]{3,2,1,0:T(8,128)(2,1)S(1)} collective-permute-done((bf16[6,1,64,256]{3,2,1,0:T(8,128)(2,1)S(1)}, bf16[6,1,64,256]{3,2,1,0:T(8,128)(2,1)S(1)}, u32[]{:S(2)}, u32[]{:S(2)}) %collective-permute-start.3) | collective-permute-done | bytes 196640 | tf_op jit(solution)/shard_map/ppermute | solution.py:16
  68.6 1.1 fusion.80
  69.7 2.0 fusion.79
  71.8 29.0 %all-gather.2.cloned.1.call-done = bf16[27,256,256]{2,1,0:T(8,128)(2,1)} async-done(((bf16[27,64,256]{2,1,0:T(8,128)(2,1)}), bf16[27,256,256]{2,1,0:T(8,128)(2,1)}) %all-gather.2.cloned.1.call-update) | async-done | bytes 3538960 | tf_op jit(solution)/shard_map/all_gather | solution.py:35
  100.8 1.3 fusion.69
  102.1 1.3 fusion.70
  103.4 1.2 convolution_add_fusion.23
  104.7 1.3 convolution_add_fusion.22
  106.0 1.2 convolution_add_fusion.21
  107.3 1.2 fusion.2
  112.3 93.4 %all-to-all-done = f32[8,1,27,256,32]{3,4,2,1,0:T(8,128)} async-done(((f32[8,1,27,256,32]{3,4,2,1,0:T(8,128)}), f32[8,1,27,256,32]{3,4,2,1,0:T(8,128)}, u32[]{:S(2)}, u32[]{:S(2)}) %all-to-all-start) | async-done | bytes 7077920 | tf_op jit(solution)/shard_map/all_to_all | solution.py:61
  205.7 3.8 %reduce_sum.9 = f32[27,256,32]{1,2,0:T(8,128)S(1)} reduce(f32[8,1,27,256,32]{3,4,2,1,0:T(8,128)} %all-to-all-done, f32[]{:T(128)} %constant.2.clone.1), dimensions={0,1}, to_apply=%region_0.1 | reduce | flops 1548288 | bytes 7962628 | tf_op jit(solution)/shard_map/reduce_sum | solution.py:66
  209.6 4.4 %copy.33 = f32[27,256,32]{2,0,1:T(8,128)} copy(f32[27,256,32]{1,2,0:T(8,128)S(1)} %reduce_sum.9) | data formatting | bytes 1769472
  214.0 4.2 %reshape.170 = f32[256,864]{1,0:T(8,128)} reshape(f32[256,27,32]{2,1,0:T(8,128)} %bitcast.419) | data formatting | bytes 1769472
  218.1 1.2 fusion.68
  219.3 1.2 convolution_add_fusion.5
  220.5 1.2 convolution_add_fusion.4
  221.7 1.2 fusion.1
  222.8 1.2 convolution_add_fusion.2
  224.0 1.2 convolution_add_fusion.1
  225.2 1.9 fusion.3
  227.0 33.5 %reduce-scatter.4.cloned.1.call-done = f32[64,864]{1,0:T(8,128)} async-done(((f32[256,864]{1,0:T(8,128)}), f32[64,864]{1,0:T(8,128)}) %reduce-scatter.4.cloned.1.call-update) | async-done | bytes 221200
  260.5 1.3 reshape.171
  262.4 0.8 broadcast_multiply_fusion
  (85 shorter events, 14.4 us)
Async XLA Ops:
  7.2 20.1 %copy-start.12 = (bf16[4,2,64,256]{3,2,1,0:T(8,128)(2,1)S(1)}, bf16[4,2,64,256]{3,2,1,0:T(8,128)(2,1)}, u32[]{:S(2)}) copy-start(bf16[4,2,64,256]{3,2,1,0:T(8,128)(2,1)} %param.6) | copy-start | bytes 786436
  8.1 6.8 %collective-permute-start.4 = (bf16[1,2,64,256]{3,2,1,0:T(8,128)(2,1)S(1)}, bf16[1,2,64,256]{3,2,1,0:T(8,128)(2,1)S(1)}, u32[]{:S(2)}, u32[]{:S(2)}) collective-permute-start(bf16[1,2,64,256]{3,2,1,0:T(8,128)(2,1)S(1)} %get-tuple-element.33), channel_id=1, source_target_pairs={{0,8},{8,16},{16,24},{1,9},{9,17},{17,25},{2,10},{10,18},{18,26},{... | collective-permute-start | bytes 196616 | tf_op jit(solution)/shard_map/ppermute | solution.py:15
  13.0 6.2 %collective-permute-start.5 = (bf16[1,2,64,256]{3,2,1,0:T(8,128)(2,1)S(1)}, bf16[1,2,64,256]{3,2,1,0:T(8,128)(2,1)S(1)}, u32[]{:S(2)}, u32[]{:S(2)}) collective-permute-start(bf16[1,2,64,256]{3,2,1,0:T(8,128)(2,1)S(1)} %get-tuple-element.32), channel_id=1, source_target_pairs={{8,0},{16,8},{24,16},{9,1},{17,9},{25,17},{10,2},{18,10},{26,18},{... | collective-permute-start | bytes 196616 | tf_op jit(solution)/shard_map/ppermute | solution.py:16
  19.2 3.8 %collective-permute-start.6 = (bf16[6,1,64,256]{3,2,1,0:T(8,128)(2,1)S(1)}, bf16[6,1,64,256]{3,2,1,0:T(8,128)(2,1)S(1)}, u32[]{:S(2)}, u32[]{:S(2)}) collective-permute-start(bf16[6,1,64,256]{3,2,1,0:T(8,128)(2,1)S(1)} %get-tuple-element.26), channel_id=1, source_target_pairs={{0,1},{1,2},{2,3},{3,4},{4,5},{5,6},{6,7},{8,9},{9,10},{10,11},{11... | collective-permute-start | bytes 589832 | tf_op jit(solution)/shard_map/ppermute | solution.py:15
  20.5 5.1 %collective-permute-start.7 = (bf16[6,1,64,256]{3,2,1,0:T(8,128)(2,1)S(1)}, bf16[6,1,64,256]{3,2,1,0:T(8,128)(2,1)S(1)}, u32[]{:S(2)}, u32[]{:S(2)}) collective-permute-start(bf16[6,1,64,256]{3,2,1,0:T(8,128)(2,1)S(1)} %get-tuple-element.27), channel_id=1, source_target_pairs={{1,0},{2,1},{3,2},{4,3},{5,4},{6,5},{7,6},{9,8},{10,9},{11,10},{12... | collective-permute-start | bytes 589832 | tf_op jit(solution)/shard_map/ppermute | solution.py:16
  41.9 163.8 %all-to-all-start = ((f32[8,1,27,256,32]{3,4,2,1,0:T(8,128)}), f32[8,1,27,256,32]{3,4,2,1,0:T(8,128)}, u32[]{:S(2)}, u32[]{:S(2)}) async-start(f32[8,1,27,256,32]{3,4,2,1,0:T(8,128)} %fusion.31), calls=%async_computation | async-start | bytes 14155776 | tf_op jit(solution)/shard_map/all_to_all | solution.py:61
  49.5 51.2 %all-gather.2.cloned.1.call-start = ((), (), s32[]{:S(2)}) async-start(), calls=%async_computation.2 | async-start | bytes 4423680 | tf_op jit(solution)/shard_map/all_gather | solution.py:35
  50.3 210.2 %reduce-scatter.4.cloned.1.call-start = ((), (), s32[]{:S(2)}) async-start(), calls=%async_computation.3 | async-start | bytes 1146880
  50.3 6.4 %collective-permute-start = (bf16[1,2,64,256]{3,2,1,0:T(8,128)(2,1)S(1)}, bf16[1,2,64,256]{3,2,1,0:T(8,128)(2,1)S(1)}, u32[]{:S(2)}, u32[]{:S(2)}) collective-permute-start(bf16[1,2,64,256]{3,2,1,0:T(8,128)(2,1)S(1)} %get-tuple-element.36), channel_id=1, source_target_pairs={{0,8},{8,16},{16,24},{1,9},{9,17},{17,25},{2,10},{10,18},{18,26},{... | collective-permute-start | bytes 196616 | tf_op jit(solution)/shard_map/ppermute | solution.py:15
  54.6 6.8 %collective-permute-start.1 = (bf16[1,2,64,256]{3,2,1,0:T(8,128)(2,1)S(1)}, bf16[1,2,64,256]{3,2,1,0:T(8,128)(2,1)S(1)}, u32[]{:S(2)}, u32[]{:S(2)}) collective-permute-start(bf16[1,2,64,256]{3,2,1,0:T(8,128)(2,1)S(1)} %get-tuple-element.37), channel_id=1, source_target_pairs={{8,0},{16,8},{24,16},{9,1},{17,9},{25,17},{10,2},{18,10},{26,18},{... | collective-permute-start | bytes 196616 | tf_op jit(solution)/shard_map/ppermute | solution.py:16
  61.5 3.7 %collective-permute-start.2 = (bf16[6,1,64,256]{3,2,1,0:T(8,128)(2,1)S(1)}, bf16[6,1,64,256]{3,2,1,0:T(8,128)(2,1)S(1)}, u32[]{:S(2)}, u32[]{:S(2)}) collective-permute-start(bf16[6,1,64,256]{3,2,1,0:T(8,128)(2,1)S(1)} %get-tuple-element.30), channel_id=1, source_target_pairs={{0,1},{1,2},{2,3},{3,4},{4,5},{5,6},{6,7},{8,9},{9,10},{10,11},{11... | collective-permute-start | bytes 589832 | tf_op jit(solution)/shard_map/ppermute | solution.py:15
  63.7 4.4 %collective-permute-start.3 = (bf16[6,1,64,256]{3,2,1,0:T(8,128)(2,1)S(1)}, bf16[6,1,64,256]{3,2,1,0:T(8,128)(2,1)S(1)}, u32[]{:S(2)}, u32[]{:S(2)}) collective-permute-start(bf16[6,1,64,256]{3,2,1,0:T(8,128)(2,1)S(1)} %get-tuple-element.31), channel_id=1, source_target_pairs={{1,0},{2,1},{3,2},{4,3},{5,4},{6,5},{7,6},{9,8},{10,9},{11,10},{12... | collective-permute-start | bytes 589832 | tf_op jit(solution)/shard_map/ppermute | solution.py:16
  100.7 7.8 %copy-start = (bf16[27,256,256]{2,1,0:T(8,128)(2,1)S(1)}, bf16[27,256,256]{2,1,0:T(8,128)(2,1)}, u32[]{:S(2)}) copy-start(bf16[27,256,256]{2,1,0:T(8,128)(2,1)} %all-gather.2.cloned.1.call-done) | copy-start | bytes 10616836
  100.7 7.8 %copy-start.11 = (bf16[4,2,64,256]{3,2,1,0:T(8,128)(2,1)S(1)}, bf16[4,2,64,256]{3,2,1,0:T(8,128)(2,1)}, u32[]{:S(2)}) copy-start(bf16[4,2,64,256]{3,2,1,0:T(8,128)(2,1)} %get-tuple-element.15) | copy-start | bytes 786436
  100.8 8.0 %copy-start.6 = (bf16[4,2,64,256]{3,2,1,0:T(8,128)(2,1)S(1)}, bf16[4,2,64,256]{3,2,1,0:T(8,128)(2,1)}, u32[]{:S(2)}) copy-start(bf16[4,2,64,256]{3,2,1,0:T(8,128)(2,1)} %get-tuple-element.22) | copy-start | bytes 786436
  100.8 8.3 %copy-start.10 = (bf16[4,2,64,256]{3,2,1,0:T(8,128)(2,1)S(1)}, bf16[4,2,64,256]{3,2,1,0:T(8,128)(2,1)}, u32[]{:S(2)}) copy-start(bf16[4,2,64,256]{3,2,1,0:T(8,128)(2,1)} %get-tuple-element.14) | copy-start | bytes 786436
  100.8 8.6 %copy-start.9 = (bf16[4,2,64,256]{3,2,1,0:T(8,128)(2,1)S(1)}, bf16[4,2,64,256]{3,2,1,0:T(8,128)(2,1)}, u32[]{:S(2)}) copy-start(bf16[4,2,64,256]{3,2,1,0:T(8,128)(2,1)} %get-tuple-element.13) | copy-start | bytes 786436
  100.8 8.9 %copy-start.3 = (bf16[4,2,64,256]{3,2,1,0:T(8,128)(2,1)S(1)}, bf16[4,2,64,256]{3,2,1,0:T(8,128)(2,1)}, u32[]{:S(2)}) copy-start(bf16[4,2,64,256]{3,2,1,0:T(8,128)(2,1)} %get-tuple-element.39) | copy-start | bytes 786436
  102.1 7.8 %copy-start.8 = (bf16[4,2,64,256]{3,2,1,0:T(8,128)(2,1)S(1)}, bf16[4,2,64,256]{3,2,1,0:T(8,128)(2,1)}, u32[]{:S(2)}) copy-start(bf16[4,2,64,256]{3,2,1,0:T(8,128)(2,1)} %get-tuple-element.12) | copy-start | bytes 786436
  104.7 5.5 %copy-start.7 = (bf16[4,2,64,256]{3,2,1,0:T(8,128)(2,1)S(1)}, bf16[4,2,64,256]{3,2,1,0:T(8,128)(2,1)}, u32[]{:S(2)}) copy-start(bf16[4,2,64,256]{3,2,1,0:T(8,128)(2,1)} %get-tuple-element.11) | copy-start | bytes 786436
  107.2 3.5 %copy-start.5 = (bf16[4,2,64,256]{3,2,1,0:T(8,128)(2,1)S(1)}, bf16[4,2,64,256]{3,2,1,0:T(8,128)(2,1)}, u32[]{:S(2)}) copy-start(bf16[4,2,64,256]{3,2,1,0:T(8,128)(2,1)} %get-tuple-element.10) | copy-start | bytes 786436
  107.3 3.7 %copy-start.4 = (bf16[4,2,64,256]{3,2,1,0:T(8,128)(2,1)S(1)}, bf16[4,2,64,256]{3,2,1,0:T(8,128)(2,1)}, u32[]{:S(2)}) copy-start(bf16[4,2,64,256]{3,2,1,0:T(8,128)(2,1)} %get-tuple-element.9) | copy-start | bytes 786436
  108.8 2.7 %copy-start.2 = (bf16[4,2,64,256]{3,2,1,0:T(8,128)(2,1)S(1)}, bf16[4,2,64,256]{3,2,1,0:T(8,128)(2,1)}, u32[]{:S(2)}) copy-start(bf16[4,2,64,256]{3,2,1,0:T(8,128)(2,1)} %get-tuple-element.8) | copy-start | bytes 786436
  109.4 2.7 %copy-start.1 = (bf16[4,2,64,256]{3,2,1,0:T(8,128)(2,1)S(1)}, bf16[4,2,64,256]{3,2,1,0:T(8,128)(2,1)}, u32[]{:S(2)}) copy-start(bf16[4,2,64,256]{3,2,1,0:T(8,128)(2,1)} %get-tuple-element.40) | copy-start | bytes 786436
Sparse Core Ops, SparseCore 0:
  52.2 48.5 all-gather.1
  218.3 42.2 reduce-scatter.3
